TPU v7x, 256 devices: a whole 4x4x8 slice. The times are simulated.
256 devices in a mesh: req: 32 (over y, x, core), tp: 8 (over z).
Axes of the slice: x: 4, y: 4, z: 8, core: 2. Of those that a mesh axis runs over, the one named last changes fastest.
Arguments:
- tokens: bfloat16 [32, 768, 2048], P('req', None, 'tp'), may hold values from -6 to 6
- q_weight: bfloat16 [2048, 2048], P(None, 'tp'), may hold values from -0.125 to 0.125
- k_weight: bfloat16 [2048, 2048], P(None, 'tp'), may hold values from -0.125 to 0.125
- v_weight: bfloat16 [2048, 2048], P(None, 'tp'), may hold values from -0.125 to 0.125
- o_weight: bfloat16 [2048, 2048], P('tp'), may hold values from -0.125 to 0.125
- q_gain: bfloat16 [2048], P('tp'), may hold values from 0.099609375 to 1.8984375
- k_gain: bfloat16 [2048], P('tp'), may hold values from 0.099609375 to 1.8984375
- post_gain: bfloat16 [2048], P('tp'), may hold values from 0.099609375 to 1.8984375
- key_pool: bfloat16 [1024, 128, 2048], P('req', None, 'tp'), may hold values from -400 to 400
- value_pool: bfloat16 [1024, 128, 2048], P('req', None, 'tp'), may hold values from -6 to 6
- cache_len: int32 [32], replicated, may hold values from 1 to 4096, as said below
- page_table: int32 [32, 32], replicated, may hold values from -1 to 1023, as said below
Outputs:
- mixed: bfloat16 [32, 768, 2048], P('req', None, 'tp')
- new_keys: bfloat16 [32, 768, 2048], P('req', None, 'tp')
- new_values: bfloat16 [32, 768, 2048], P('req', None, 'tp')
Inputs may be any that keep to these rules, and one draw needn't show every extreme that they name: `cache_len`: on some index of req the one request hold 4096 cached tokens. `page_table`: entry p of request r is a pool page (index d * 32 + local page of index d of req) for p < ceil(cache_len[r] / 128) and -1 otherwise; no pool page is named twice; the pages named by the requests of one index of req lie at most 1 on any one index of req, and some pair of indices reaches 1.
All inputs are finite; a program needn't handle non-finite values.
Results may differ from a plain program's by a relative error of at most 0.013.
Values may be sent and summed in bfloat16 or wider, within the bound.
No kernel may reach another device: no remote copies, remote signals or barrier semaphores. Data moves between devices by JAX's collectives and lax.ppermute only.
A program may use at most 64 MiB of HBM per device.

v0:
```python
import jax
import jax.numpy as jnp
from jax import lax
from jax.sharding import PartitionSpec as P

HEAD_DIM = 128
EPSILON = 1e-06
ROPE_BASE = 500000.0


def rotate(values, positions):
    half_dim = values.shape[-1] // 2
    freqs = jnp.power(
        jnp.float32(ROPE_BASE), -jnp.arange(half_dim, dtype=jnp.float32) * 2.0 / values.shape[-1]
    )
    angles = positions[..., None] * freqs
    cosine = jnp.cos(angles)[..., None, :]
    sine_part = jnp.sin(angles)[..., None, :]
    first_half = values[..., :half_dim]
    second_half = values[..., half_dim:]
    return jnp.concatenate(
        [
            first_half * cosine - second_half * sine_part,
            second_half * cosine + first_half * sine_part,
        ],
        -1,
    )


def page_slots(page_table, pool_dev):
    valid = page_table >= 0
    source = jnp.where(valid, page_table // pool_dev, -1)
    local = jnp.where(valid, page_table % pool_dev, 0)
    order = jnp.arange(page_table.shape[1])
    same = (
        (source[:, :, None] == source[:, None, :])
        & valid[:, None, :]
        & (order[None, :, None] > order[None, None, :])
    )
    rank = jnp.sum(same.astype(jnp.int32), -1)
    return (source, rank, valid, local)


def attend(query, cache_k, cache_v, fresh_k, fresh_v, lengths):
    scale = query.shape[-1] ** (-0.5)
    req_dev, block_len, heads_here, head_dim = query.shape
    cache_span = cache_k.shape[1]
    cache_mask = (jnp.arange(cache_span)[None, :] < lengths[:, None])[:, None, :]
    causal = (jnp.arange(block_len)[:, None] >= jnp.arange(block_len)[None, :])[None]

    def one_head(head):
        query_h = lax.dynamic_index_in_dim(query, head, 2, keepdims=False)
        cache_kh = lax.dynamic_index_in_dim(cache_k, head, 2, keepdims=False)
        cache_vh = lax.dynamic_index_in_dim(cache_v, head, 2, keepdims=False)
        fresh_kh = lax.dynamic_index_in_dim(fresh_k, head, 2, keepdims=False)
        fresh_vh = lax.dynamic_index_in_dim(fresh_v, head, 2, keepdims=False)
        cache_scores = (
            jnp.einsum("rqd,rkd->rqk", query_h, cache_kh, preferred_element_type=jnp.float32)
            * scale
        )
        fresh_scores = (
            jnp.einsum("rqd,rkd->rqk", query_h, fresh_kh, preferred_element_type=jnp.float32)
            * scale
        )
        scores = jnp.concatenate(
            [jnp.where(cache_mask, cache_scores, -1e30), jnp.where(causal, fresh_scores, -1e30)], -1
        )
        peak = jnp.max(scores, -1, keepdims=True)
        raised = jnp.exp(scores - peak)
        weights = (raised / jnp.sum(raised, -1, keepdims=True)).astype(jnp.bfloat16)
        result = jnp.einsum(
            "rqk,rkd->rqd", weights[..., :cache_span], cache_vh, preferred_element_type=jnp.float32
        )
        result = result + jnp.einsum(
            "rqk,rkd->rqd", weights[..., cache_span:], fresh_vh, preferred_element_type=jnp.float32
        )
        return result.astype(jnp.bfloat16)

    per_head = lax.map(one_head, jnp.arange(heads_here, dtype=jnp.int32))
    return jnp.transpose(per_head, (1, 2, 0, 3)).reshape(req_dev, block_len, heads_here * head_dim)


def body(
    tokens,
    q_weight,
    k_weight,
    v_weight,
    o_weight,
    q_gain,
    k_gain,
    post_gain,
    key_pool,
    value_pool,
    cache_len,
    page_table,
):
    req_dev, block_len, feature_part = tokens.shape
    model_width = q_weight.shape[0]
    columns = q_weight.shape[1]
    heads_here = columns // HEAD_DIM
    owners = lax.axis_size("req")
    owner = lax.axis_index("req")
    tensor_size = lax.axis_size("tp")
    row_count = req_dev * block_len
    flat = tokens.reshape(row_count, feature_part)
    empty = jnp.zeros((row_count, columns), jnp.float32)
    totals = (empty, empty, empty)
    piece = lax.all_gather(flat, "tp", axis=1, tiled=True)
    result = []
    for total, weight in zip(totals, (q_weight, k_weight, v_weight)):
        result.append(jnp.dot(piece, weight, preferred_element_type=jnp.float32))
    q_proj, k_proj, v_proj = tuple(result)
    q_squares, k_squares = lax.psum(
        (jnp.sum(q_proj * q_proj, 1), jnp.sum(k_proj * k_proj, 1)), "tp"
    )
    full_columns = columns * tensor_size
    q_normed = (
        q_proj * lax.rsqrt(q_squares / full_columns + EPSILON)[:, None] * q_gain.astype(jnp.float32)
    )
    k_normed = (
        k_proj * lax.rsqrt(k_squares / full_columns + EPSILON)[:, None] * k_gain.astype(jnp.float32)
    )
    lengths = lax.dynamic_slice_in_dim(cache_len, owner * req_dev, req_dev)
    positions = (lengths[:, None] + jnp.arange(block_len, dtype=jnp.int32)[None, :]).astype(
        jnp.float32
    )
    query = rotate(q_normed.reshape(req_dev, block_len, heads_here, HEAD_DIM), positions).astype(
        jnp.bfloat16
    )
    new_keys = rotate(k_normed.reshape(req_dev, block_len, heads_here, HEAD_DIM), positions).astype(
        jnp.bfloat16
    )
    new_values = v_proj.astype(jnp.bfloat16).reshape(req_dev, block_len, heads_here, HEAD_DIM)
    pool_dev = key_pool.shape[0]
    page_len = key_pool.shape[1]
    pair_cap = pool_dev // owners
    source, rank, valid, local = page_slots(page_table, pool_dev)
    match = (
        valid[:, None, :]
        & (source[:, None, :] == owner)
        & (rank[:, None, :] == jnp.arange(pair_cap)[None, :, None])
    )
    chosen = jnp.sum(jnp.where(match, local[:, None, :], 0), -1).reshape(-1)
    outgoing_k = key_pool[chosen]
    outgoing_v = value_pool[chosen]
    arrived_k, arrived_v = (
        lax.all_to_all(outgoing_k, "req", split_axis=0, concat_axis=0, tiled=True),
        lax.all_to_all(outgoing_v, "req", split_axis=0, concat_axis=0, tiled=True),
    )
    mine_source = lax.dynamic_index_in_dim(source, owner, 0, keepdims=False)
    mine_rank = lax.dynamic_index_in_dim(rank, owner, 0, keepdims=False)
    mine_valid = lax.dynamic_index_in_dim(valid, owner, 0, keepdims=False)
    placement = jnp.where(mine_valid, mine_source * pair_cap + mine_rank, 0)
    cache_span = page_table.shape[1] * page_len
    cache_k = arrived_k[placement].reshape(req_dev, cache_span, heads_here, HEAD_DIM)
    cache_v = arrived_v[placement].reshape(req_dev, cache_span, heads_here, HEAD_DIM)
    attended = attend(query, cache_k, cache_v, new_keys, new_values, lengths)
    partial_value = jnp.dot(
        attended.reshape(row_count, columns), o_weight, preferred_element_type=jnp.float32
    )
    summed = lax.psum(partial_value.astype(jnp.bfloat16), "tp").astype(jnp.float32)
    squares = jnp.sum(summed * summed, 1)
    normed_all = summed * lax.rsqrt(squares / model_width + EPSILON)[:, None]
    normed = lax.dynamic_slice_in_dim(
        normed_all, lax.axis_index("tp") * feature_part, feature_part, 1
    )
    mixed = (flat.astype(jnp.float32) + normed * post_gain.astype(jnp.float32)).astype(jnp.bfloat16)
    return (
        mixed.reshape(req_dev, block_len, feature_part),
        new_keys.reshape(req_dev, block_len, columns),
        new_values.reshape(req_dev, block_len, columns),
    )


def solution(mesh):
    placed = (
        P("req", None, "tp"),
        P(None, "tp"),
        P(None, "tp"),
        P(None, "tp"),
        P("tp", None),
        P("tp"),
        P("tp"),
        P("tp"),
        P("req", None, "tp"),
        P("req", None, "tp"),
        P(),
        P(),
    )
    return jax.shard_map(
        body,
        mesh=mesh,
        in_specs=placed,
        out_specs=(P("req", None, "tp"), P("req", None, "tp"), P("req", None, "tp")),
        check_vma=False,
    )
```

profile of v0, /device:TPU:1, one launch (start us, length us, event | category | flops | bytes accessed | tf_op | source)
XLA Modules:
  0.0 275.5 jit_solution(12910835094052155758)
XLA Ops:
  11.1 2.0 gather_fusion
  13.1 8.6 %all-to-all-start = ((bf16[32,128,256]{2,1,0:T(8,128)(2,1)}), bf16[32,128,256]{2,1,0:T(8,128)(2,1)S(1)}, u32[]{:S(2)}, u32[]{:S(2)}) async-start(bf16[32,128,256]{2,1,0:T(8,128)(2,1)} %gather_fusion), calls=%async_computation | async-start | bytes 4194304 | tf_op jit(solution)/shard_map/all_to_all | solution.py:147
  21.7 3.6 %gather_fusion.2 = bf16[32,128,256]{2,1,0:T(8,128)(2,1)} fusion(bf16[32,128,256]{2,1,0:T(8,128)(2,1)} %param.23, s32[1024]{0:T(1024)S(1)} %pad_clamp_fusion.1), kind=kCustom, calls=%fused_computation.2 | custom fusion | bytes 4194432 | tf_op jit(solution)/shard_map/gather | solution.py:145
  25.3 25.0 %all-to-all-done = bf16[32,128,256]{2,1,0:T(8,128)(2,1)S(1)} async-done(((bf16[32,128,256]{2,1,0:T(8,128)(2,1)}), bf16[32,128,256]{2,1,0:T(8,128)(2,1)S(1)}, u32[]{:S(2)}, u32[]{:S(2)}) %all-to-all-start) | async-done | bytes 2097184 | tf_op jit(solution)/shard_map/all_to_all | solution.py:147
  50.3 6.0 %all-to-all-start.1 = ((bf16[32,128,256]{2,1,0:T(8,128)(2,1)}), bf16[32,128,256]{2,1,0:T(8,128)(2,1)}, u32[]{:S(2)}, u32[]{:S(2)}) async-start(bf16[32,128,256]{2,1,0:T(8,128)(2,1)} %gather_fusion.2), calls=%async_computation.1 | async-start | bytes 4194304 | tf_op jit(solution)/shard_map/all_to_all | solution.py:148
  59.1 2.1 gather_fusion.1
  61.1 3.9 %reshape.515 = bf16[1,4096,2,128]{3,2,1,0:T(2,128)(2,1)} reshape(bf16[32,128,256]{2,1,0:T(8,128)(2,1)} %gather_fusion.1) | data formatting | bytes 4194304 | tf_op jit(solution)/shard_map/reshape | solution.py:155
  65.1 1.9 copy.51
  66.9 17.7 %all-to-all-done.1 = bf16[32,128,256]{2,1,0:T(8,128)(2,1)} async-done(((bf16[32,128,256]{2,1,0:T(8,128)(2,1)}), bf16[32,128,256]{2,1,0:T(8,128)(2,1)}, u32[]{:S(2)}, u32[]{:S(2)}) %all-to-all-start.1) | async-done | bytes 2097184 | tf_op jit(solution)/shard_map/all_to_all | solution.py:148
  84.7 3.6 %gather_fusion.3 = bf16[32,128,256]{2,1,0:T(8,128)(2,1)} fusion(bf16[32,128,256]{2,1,0:T(8,128)(2,1)} %all-to-all-done.1, s32[1024]{0:T(1024)S(1)} %pad_clamp_fusion), kind=kCustom, calls=%fused_computation.3 | custom fusion | bytes 4194432 | tf_op jit(solution)/shard_map/gather | solution.py:156
  88.3 4.0 %reshape.516 = bf16[1,4096,2,128]{3,2,1,0:T(2,128)(2,1)} reshape(bf16[32,128,256]{2,1,0:T(8,128)(2,1)} %gather_fusion.3) | data formatting | bytes 4194304 | tf_op jit(solution)/shard_map/reshape | solution.py:156
  92.3 3.2 %copy.52 = bf16[1,4096,2,128]{3,1,2,0:T(8,128)(2,1)} copy(bf16[1,4096,2,128]{3,2,1,0:T(2,128)(2,1)} %reshape.516) | data formatting | bytes 4194304
  95.5 4.3 %multiply_reduce_fusion.2 = (f32[768]{0:T(1024)S(1)}, f32[768,256]{0,1:T(8,128)}) fusion(bf16[2048,256]{1,0:T(8,128)(2,1)} %param.15, bf16[1,768,2048]{2,1,0:T(8,128)(2,1)} %all-gather.3.cloned.1.call-done), kind=kOutput, calls=%fused_computation.65 | convolution fusion | flops 805698816 | bytes 4983808 | tf_op jit(solution)/shard_map/dot_general | solution.py:111
  99.7 2.0 multiply_reduce_fusion.1
  101.7 16.7 %all-reduce = (f32[768]{0:T(1024)S(1)}, f32[768]{0:T(1024)S(1)}) all-reduce(f32[768]{0:T(1024)S(1)} %get-tuple-element.160, f32[768]{0:T(1024)S(1)} %get-tuple-element.162), channel_id=1, replica_groups=mesh['req'=32,'tp'=8] {'tp'}, use_global_device_ids=true, to_apply=%region_1.0 | all-reduce | flops 1536 | bytes 12288 | tf_op jit(solution)/shard_map/psum | solution.py:113
  120.5 2.2 copy.67
  125.9 2.2 copy.65
  129.3 1.7 multiply_subtract_fusion
  133.5 1.8 fusion.38
  135.3 34.6 %while.11 = (s32[]{:T(128)}, bf16[2,1,768,128]{2,3,0,1:T(8,128)(2,1)}, s32[2]{0:T(128)S(1)}, bf16[1,768,2,128]{3,1,2,0:T(8,128)(2,1)S(1)}, bf16[1,4096,2,128]{3,...) while((s32[]{:T(128)}, ...), condition=%wide.region_10.11_spmd.clone, body=%wide.region_6.10_spmd.clone.sunk | while | flops 1950747136 | bytes 74421992 | solution.py:79
  138.2 2.2 fusion.89
  141.9 4.4 %fusion.90 = f32[768]{0:T(1024)S(1)} fusion(f32[1,768,768]{2,1,0:T(8,128)S(1)} %get-tuple-element.227, f32[1,768,4096]{2,1,0:T(8,128)S(1)} %get-tuple-element.228, f32[768]{0:T(1024)S(1)} %reduce_max.30), kind=kLoop, calls=%fused_computation.12.clone.1 | loop fusion | flops 11205888 | bytes 14948352 | tf_op jit(solution)/shard_map/while/body/eval_jaxpr/reduce_sum | solution.py:70
  146.3 3.1 %divide_convert_fusion.2 = bf16[1,768,4864]{2,1,0:T(8,128)(2,1)S(1)} fusion(f32[1,768,768]{2,1,0:T(8,128)S(1)} %get-tuple-element.227, f32[1,768,4096]{2,1,0:T(8,128)S(1)} %get-tuple-element.228, f32[768]{0:T(1024)S(1)} %fusion.90, f32[768]{0:T(1024)S(1)} %reduce_max.30), kind=kLoop, calls=%fused_computation.8.clone.1 | loop fusion | flops 14942208 | bytes 22419456 | tf_op jit(solution)/shard_map/while/body/eval_jaxpr/convert_element_type | solution.py:70
  149.5 1.8 fusion.91
  155.5 2.2 fusion.89
  157.7 1.5 fusion.88
  159.2 4.4 %fusion.90 = f32[768]{0:T(1024)S(1)} fusion(f32[1,768,768]{2,1,0:T(8,128)S(1)} %get-tuple-element.227, f32[1,768,4096]{2,1,0:T(8,128)S(1)} %get-tuple-element.228, f32[768]{0:T(1024)S(1)} %reduce_max.30), kind=kLoop, calls=%fused_computation.12.clone.1 | loop fusion | flops 11205888 | bytes 14948352 | tf_op jit(solution)/shard_map/while/body/eval_jaxpr/reduce_sum | solution.py:70
  163.6 3.1 %divide_convert_fusion.2 = bf16[1,768,4864]{2,1,0:T(8,128)(2,1)S(1)} fusion(f32[1,768,768]{2,1,0:T(8,128)S(1)} %get-tuple-element.227, f32[1,768,4096]{2,1,0:T(8,128)S(1)} %get-tuple-element.228, f32[768]{0:T(1024)S(1)} %fusion.90, f32[768]{0:T(1024)S(1)} %reduce_max.30), kind=kLoop, calls=%fused_computation.8.clone.1 | loop fusion | flops 14942208 | bytes 22419456 | tf_op jit(solution)/shard_map/while/body/eval_jaxpr/convert_element_type | solution.py:70
  166.8 1.8 fusion.91
  169.9 4.0 %convolution_convert_fusion = bf16[768,2048]{1,0:T(8,128)(2,1)} fusion(bf16[768,256]{0,1:T(8,128)(2,1)} %bitcast.119, bf16[256,2048]{1,0:T(8,128)(2,1)} %param.18), kind=kOutput, calls=%fused_computation.45 | convolution fusion | flops 806879232 | bytes 4587520 | tf_op jit(solution)/shard_map/dot_general | solution.py:158
  176.8 87.0 %all-reduce.3.cloned.1.call-done = bf16[768,2048]{1,0:T(8,128)(2,1)} async-done(((bf16[768,2048]{1,0:T(8,128)(2,1)}), bf16[768,2048]{1,0:T(8,128)(2,1)}) %all-reduce.3.cloned.1.call-update) | async-done | bytes 3145744 | tf_op jit(solution)/shard_map/psum | solution.py:161
  263.8 2.7 multiply_reduce_fusion
  (92 shorter events, 26.9 us)
Async XLA Ops:
  7.2 3.9 %copy-start = (bf16[32,128,256]{2,1,0:T(8,128)(2,1)S(1)}, bf16[32,128,256]{2,1,0:T(8,128)(2,1)}, u32[]{:S(2)}) copy-start(bf16[32,128,256]{2,1,0:T(8,128)(2,1)} %param.22) | copy-start | bytes 6291460
  7.2 88.3 %all-gather.3.cloned.1.call-start = ((), (), s32[]{:S(2)}) async-start(), calls=%async_computation.3 | async-start | bytes 3538944 | tf_op jit(solution)/shard_map/all_gather | solution.py:108
  13.1 37.2 %all-to-all-start = ((bf16[32,128,256]{2,1,0:T(8,128)(2,1)}), bf16[32,128,256]{2,1,0:T(8,128)(2,1)S(1)}, u32[]{:S(2)}, u32[]{:S(2)}) async-start(bf16[32,128,256]{2,1,0:T(8,128)(2,1)} %gather_fusion), calls=%async_computation | async-start | bytes 4194304 | tf_op jit(solution)/shard_map/all_to_all | solution.py:147
  25.3 31.1 %copy-start.15 = (bf16[256]{0:T(256)(128)(2,1)S(1)}, bf16[256]{0:T(256)(128)(2,1)}, u32[]{:S(2)}) copy-start(bf16[256]{0:T(256)(128)(2,1)} %param.20) | copy-start | bytes 1540
  25.3 31.1 %copy-start.16 = (bf16[256]{0:T(256)(128)(2,1)S(1)}, bf16[256]{0:T(256)(128)(2,1)}, u32[]{:S(2)}) copy-start(bf16[256]{0:T(256)(128)(2,1)} %param.19) | copy-start | bytes 1540
  25.3 31.1 %copy-start.17 = (s32[32]{0:T(128)S(1)}, s32[32]{0:T(128)}, u32[]{:S(2)}) copy-start(s32[32]{0:T(128)} %param.24) | copy-start | bytes 388
  50.3 34.4 %all-to-all-start.1 = ((bf16[32,128,256]{2,1,0:T(8,128)(2,1)}), bf16[32,128,256]{2,1,0:T(8,128)(2,1)}, u32[]{:S(2)}, u32[]{:S(2)}) async-start(bf16[32,128,256]{2,1,0:T(8,128)(2,1)} %gather_fusion.2), calls=%async_computation.1 | async-start | bytes 4194304 | tf_op jit(solution)/shard_map/all_to_all | solution.py:148
  56.3 207.5 %all-reduce.3.cloned.1.call-start = ((), (), s32[]{:S(2)}) async-start(), calls=%async_computation.2 | async-start | bytes 6291456 | tf_op jit(solution)/shard_map/psum | solution.py:161
  95.5 4.3 %copy-start.11 = (bf16[1,768,2048]{2,1,0:T(8,128)(2,1)S(1)}, bf16[1,768,2048]{2,1,0:T(8,128)(2,1)}, u32[]{:S(2)}) copy-start(bf16[1,768,2048]{2,1,0:T(8,128)(2,1)} %all-gather.3.cloned.1.call-done) | copy-start | bytes 9437188
  95.5 4.3 %copy-start.13 = (bf16[2048,256]{1,0:T(8,128)(2,1)S(1)}, bf16[2048,256]{1,0:T(8,128)(2,1)}, u32[]{:S(2)}) copy-start(bf16[2048,256]{1,0:T(8,128)(2,1)} %param.16) | copy-start | bytes 3145732
  129.3 2.7 copy-start.5
  129.3 2.7 copy-start.6
  131.0 1.2 copy-start.3
  131.0 2.2 copy-start.12
  131.0 2.5 copy-start.14
  146.3 3.2 %copy-start.7 = (bf16[1,4096,2,128]{3,1,2,0:T(8,128)(2,1)S(1)}, bf16[1,4096,2,128]{3,1,2,0:T(8,128)(2,1)}, u32[]{:S(2)}) copy-start(bf16[1,4096,2,128]{3,1,2,0:T(8,128)(2,1)} %get-tuple-element.261) | copy-start | bytes 6291460 | tf_op jit(solution)/shard_map/while
  149.5 1.8 copy-start.9
  163.6 3.2 %copy-start.7 = (bf16[1,4096,2,128]{3,1,2,0:T(8,128)(2,1)S(1)}, bf16[1,4096,2,128]{3,1,2,0:T(8,128)(2,1)}, u32[]{:S(2)}) copy-start(bf16[1,4096,2,128]{3,1,2,0:T(8,128)(2,1)} %get-tuple-element.261) | copy-start | bytes 6291460 | tf_op jit(solution)/shard_map/while
  166.8 1.8 copy-start.9
  174.0 0.7 copy-start.18
  174.0 1.0 copy-start.10
  174.0 1.9 copy-start.4
  263.8 2.8 %copy-start.2 = (bf16[768,2048]{1,0:T(8,128)(2,1)S(1)}, bf16[768,2048]{1,0:T(8,128)(2,1)}, u32[]{:S(2)}) copy-start(bf16[768,2048]{1,0:T(8,128)(2,1)} %all-reduce.3.cloned.1.call-done) | copy-start | bytes 9437188
  266.7 1.0 copy-start.8
  266.7 1.9 copy-start.1
Sparse Core Ops, SparseCore 0:
  9.7 54.7 all-gather.2
  174.1 89.6 all-reduce.2
where the time goes:
time: 276 us; the launch traced here: 275 us
  waiting for transfers between devices  130 us (47%)
  local copies, waits for them, and re-layouts  39.3 us (14%)
  other arithmetic  32.5 us (12%)
  matrix products  24 us (9%)
  blocking collectives  16.7 us (6%)
  starting transfers between devices  14.7 us (5%)
  between operations  14.3 us (5%)
  loops' own time  3.58 us (1%)
    psum x1, waiting for transfers between devices, body(): lax.psum(partial_value.astype(jnp.bfloat16), 'tp').astype(jnp.float32)  87 us
    all_to_all x1, waiting for transfers between devices, body(): lax.all_to_all(outgoing_k, 'req', split_axis=0, concat_axis=0, tiled=True)  25 us
    all_to_all x1, waiting for transfers between devices, body(): lax.all_to_all(outgoing_v, 'req', split_axis=0, concat_axis=0, tiled=True)  17.7 us
    psum x1, blocking collectives, body(): lax.psum((jnp.sum(q_proj * q_proj, 1), jnp.sum(k_proj * k_proj, 1)), 'tp')  16.7 us
    unnamed x41, local copies, waits for them, and re-layouts  15 us
    reduce_sum x2, other arithmetic, one_head(): weights = (raised / jnp.sum(raised, -1, keepdims=True)).astype(jnp.bfloat16)  8.73 us
    all_to_all x1, starting transfers between devices, body(): lax.all_to_all(outgoing_k, 'req', split_axis=0, concat_axis=0, tiled=True)  8.58 us
    dot_general x3, matrix products, body(): result.append(jnp.dot(piece, weight, preferred_element_type=jnp.float32))  8.09 us
  transfers between devices with their start and end apart: 4, of which 3 were waited for; matrix products, arithmetic and copies ran while one was open for 12% of the time, Pallas kernels for 0%

commit v1 on v0

--- a/solution.py
+++ b/solution.py
@@ -158,7 +158,9 @@
     partial_value = jnp.dot(
         attended.reshape(row_count, columns), o_weight, preferred_element_type=jnp.float32
     )
-    summed = lax.psum(partial_value.astype(jnp.bfloat16), "tp").astype(jnp.float32)
+    summed = jnp.sum(
+        lax.all_gather(partial_value.astype(jnp.bfloat16), axis_name="tp"), axis=0
+    ).astype(jnp.float32)
     squares = jnp.sum(summed * summed, 1)
     normed_all = summed * lax.rsqrt(squares / model_width + EPSILON)[:, None]
     normed = lax.dynamic_slice_in_dim(

time: 276 us -> 448 us (1.62)
  waiting for transfers between devices: 130 us -> 292 us
  other arithmetic: 32.5 us -> 47.1 us
  local copies, waits for them, and re-layouts: 39.3 us -> 34.3 us
    all_gather x0 -> x1, waiting for transfers between devices: none -> 247 us  [body(): lax.all_gather(partial_value.astype(jnp.bfloat16), axis_name='tp')]
    psum x1 -> x0, waiting for transfers between devices: 87 us -> none  [body(): lax.psum(partial_value.astype(jnp.bfloat16), 'tp').astype(jnp.float32)]
    reduce_sum x0 -> x1, other arithmetic: none -> 15.7 us  [body(): jnp.sum(lax.all_gather(partial_value.astype(jnp.bfloat16), axis_name='tp'...]
    all_to_all x1, waiting for transfers between devices: 17.7 us -> 25 us  [body(): lax.all_to_all(outgoing_v, 'req', split_axis=0, concat_axis=0, tiled=True)]
    all_to_all x1, waiting for transfers between devices: 25 us -> 19.4 us  [body(): lax.all_to_all(outgoing_k, 'req', split_axis=0, concat_axis=0, tiled=True)]
    unnamed x41 -> x43, local copies, waits for them, and re-layouts: 15 us -> 14.4 us
  transfers between devices with their start and end apart: 4 -> 4, of which waited for: 3 -> 3; matrix products, arithmetic and copies ran while one was open for 12% -> 6% of each run, Pallas kernels for 0% -> 0%
where the time goes in v1:
time: 448 us; the launch traced here: 447 us
  waiting for transfers between devices  292 us (65%)
  other arithmetic  47.1 us (11%)
  local copies, waits for them, and re-layouts  34.3 us (8%)
  matrix products  24.1 us (5%)
  blocking collectives  16.5 us (4%)
  starting transfers between devices  14.7 us (3%)
  between operations  14.3 us (3%)
    all_gather x1, waiting for transfers between devices, body(): lax.all_gather(partial_value.astype(jnp.bfloat16), axis_name='tp')  247 us
    all_to_all x1, waiting for transfers between devices, body(): lax.all_to_all(outgoing_v, 'req', split_axis=0, concat_axis=0, tiled=True)  25 us
    all_to_all x1, waiting for transfers between devices, body(): lax.all_to_all(outgoing_k, 'req', split_axis=0, concat_axis=0, tiled=True)  19.4 us
    psum x1, blocking collectives, body(): lax.psum((jnp.sum(q_proj * q_proj, 1), jnp.sum(k_proj * k_proj, 1)), 'tp')  16.5 us
    reduce_sum x1, other arithmetic, body(): jnp.sum(lax.all_gather(partial_value.astype(jnp.bfloat16), axis_name='tp'...  15.7 us
    unnamed x43, local copies, waits for them, and re-layouts  14.4 us
  transfers between devices with their start and end apart: 4, of which 3 were waited for; matrix products, arithmetic and copies ran while one was open for 6% of the time, Pallas kernels for 0%

profile of v1, /device:TPU:1, one launch (start us, length us, event | category | flops | bytes accessed | tf_op | source)
XLA Modules:
  0.0 447.1 jit_solution(12921070034811374400)
XLA Ops:
  11.1 2.0 gather_fusion.2
  13.1 8.6 %all-to-all-start.1 = ((bf16[32,128,256]{2,1,0:T(8,128)(2,1)}), bf16[32,128,256]{2,1,0:T(8,128)(2,1)S(1)}, u32[]{:S(2)}, u32[]{:S(2)}) async-start(bf16[32,128,256]{2,1,0:T(8,128)(2,1)} %gather_fusion.2), calls=%async_computation.1 | async-start | bytes 4194304 | tf_op jit(solution)/shard_map/all_to_all | solution.py:148
  21.7 3.6 gather_fusion
  25.3 25.0 %all-to-all-done.1 = bf16[32,128,256]{2,1,0:T(8,128)(2,1)S(1)} async-done(((bf16[32,128,256]{2,1,0:T(8,128)(2,1)}), bf16[32,128,256]{2,1,0:T(8,128)(2,1)S(1)}, u32[]{:S(2)}, u32[]{:S(2)}) %all-to-all-start.1) | async-done | bytes 2097184 | tf_op jit(solution)/shard_map/all_to_all | solution.py:148
  50.2 6.1 %all-to-all-start = ((bf16[32,128,256]{2,1,0:T(8,128)(2,1)}), bf16[32,128,256]{2,1,0:T(8,128)(2,1)}, u32[]{:S(2)}, u32[]{:S(2)}) async-start(bf16[32,128,256]{2,1,0:T(8,128)(2,1)} %gather_fusion), calls=%async_computation | async-start | bytes 4194304 | tf_op jit(solution)/shard_map/all_to_all | solution.py:147
  59.0 2.0 gather_fusion.3
  61.1 2.5 reshape.517
  65.2 19.4 %all-to-all-done = bf16[32,128,256]{2,1,0:T(8,128)(2,1)} async-done(((bf16[32,128,256]{2,1,0:T(8,128)(2,1)}), bf16[32,128,256]{2,1,0:T(8,128)(2,1)}, u32[]{:S(2)}, u32[]{:S(2)}) %all-to-all-start) | async-done | bytes 2097184 | tf_op jit(solution)/shard_map/all_to_all | solution.py:147
  84.7 2.3 gather_fusion.1
  87.0 2.1 reshape.516
  89.1 1.9 copy.51
  91.0 4.3 multiply_reduce_fusion.1
  95.2 2.0 multiply_reduce_fusion.2
  97.2 16.5 %all-reduce = (f32[768]{0:T(1024)S(1)}, f32[768]{0:T(1024)S(1)}) all-reduce(f32[768]{0:T(1024)S(1)} %get-tuple-element.160, f32[768]{0:T(1024)S(1)} %get-tuple-element.162), channel_id=1, replica_groups=mesh['req'=32,'tp'=8] {'tp'}, use_global_device_ids=true, to_apply=%region_1.0 | all-reduce | flops 1536 | bytes 12288 | tf_op jit(solution)/shard_map/psum | solution.py:113
  117.0 2.1 copy.68
  119.1 2.2 copy.66
  121.3 2.2 copy.67
  124.7 1.7 multiply_subtract_fusion
  128.9 1.8 fusion.38
  130.7 35.0 %while.11 = (s32[]{:T(128)}, bf16[2,1,768,128]{2,3,0,1:T(8,128)(2,1)}, s32[2]{0:T(128)S(1)}, bf16[1,768,2,128]{3,1,2,0:T(8,128)(2,1)S(1)}, bf16[1,4096,2,128]{3,...) while((s32[]{:T(128)}, ...), condition=%wide.region_10.11_spmd.clone, body=%wide.region_6.10_spmd.clone.sunk | while | flops 1950747136 | bytes 74421496 | solution.py:79
  135.3 2.2 fusion.89
  137.5 4.4 fusion.90
  141.9 3.1 divide_convert_fusion.2
  145.1 1.8 fusion.91
  152.8 2.2 fusion.89
  155.0 4.4 fusion.90
  159.4 3.1 divide_convert_fusion.2
  162.6 1.8 fusion.91
  165.7 4.1 convolution_convert_fusion
  172.7 247.1 %all-gather.7.cloned.1.call-done = bf16[6144,2048]{1,0:T(8,128)(2,1)} async-done(((bf16[768,2048]{1,0:T(8,128)(2,1)}), bf16[6144,2048]{1,0:T(8,128)(2,1)}) %all-gather.7.cloned.1.call-update) | async-done | bytes 25165840 | tf_op jit(solution)/shard_map/all_gather | solution.py:162
  419.8 15.7 %reduce_sum.73 = bf16[768,2048]{1,0:T(8,128)(2,1)} reduce(bf16[8,768,2048]{2,1,0:T(8,128)(2,1)} %bitcast.118, bf16[]{:T(256)} %constant.91.clone.1), dimensions={0}, to_apply=%region_11.12 | reduce | flops 11010048 | bytes 28311554 | tf_op jit(solution)/shard_map/reduce_sum | solution.py:161
  435.4 2.7 multiply_reduce_fusion
  (95 shorter events, 28.0 us)
Async XLA Ops:
  7.2 3.9 copy-start
  7.2 83.8 %all-gather.5.cloned.1.call-start = ((), (), s32[]{:S(2)}) async-start(), calls=%async_computation.2 | async-start | bytes 3538944 | tf_op jit(solution)/shard_map/all_gather | solution.py:108
  13.1 37.2 %all-to-all-start.1 = ((bf16[32,128,256]{2,1,0:T(8,128)(2,1)}), bf16[32,128,256]{2,1,0:T(8,128)(2,1)S(1)}, u32[]{:S(2)}, u32[]{:S(2)}) async-start(bf16[32,128,256]{2,1,0:T(8,128)(2,1)} %gather_fusion.2), calls=%async_computation.1 | async-start | bytes 4194304 | tf_op jit(solution)/shard_map/all_to_all | solution.py:148
  25.3 31.1 %copy-start.16 = (bf16[256]{0:T(256)(128)(2,1)S(1)}, bf16[256]{0:T(256)(128)(2,1)}, u32[]{:S(2)}) copy-start(bf16[256]{0:T(256)(128)(2,1)} %param.19) | copy-start | bytes 1540
  25.3 31.1 %copy-start.17 = (bf16[256]{0:T(256)(128)(2,1)S(1)}, bf16[256]{0:T(256)(128)(2,1)}, u32[]{:S(2)}) copy-start(bf16[256]{0:T(256)(128)(2,1)} %param.20) | copy-start | bytes 1540
  25.3 31.1 %copy-start.18 = (s32[32]{0:T(128)S(1)}, s32[32]{0:T(128)}, u32[]{:S(2)}) copy-start(s32[32]{0:T(128)} %param.24) | copy-start | bytes 388
  50.2 34.4 %all-to-all-start = ((bf16[32,128,256]{2,1,0:T(8,128)(2,1)}), bf16[32,128,256]{2,1,0:T(8,128)(2,1)}, u32[]{:S(2)}, u32[]{:S(2)}) async-start(bf16[32,128,256]{2,1,0:T(8,128)(2,1)} %gather_fusion), calls=%async_computation | async-start | bytes 4194304 | tf_op jit(solution)/shard_map/all_to_all | solution.py:147
  56.3 363.5 %all-gather.7.cloned.1.call-start = ((), (), s32[]{:S(2)}) async-start(), calls=%async_computation.3 | async-start | bytes 28311552 | tf_op jit(solution)/shard_map/all_gather | solution.py:162
  90.9 4.3 copy-start.12
  91.0 4.3 copy-start.14
  113.7 2.2 copy-start.9
  124.7 2.7 copy-start.5
  124.7 2.7 copy-start.6
  126.4 1.2 copy-start.3
  126.4 2.2 copy-start.13
  126.4 2.5 copy-start.15
  141.9 3.2 copy-start.7
  145.1 1.8 copy-start.10
  159.4 3.2 copy-start.7
  162.6 1.8 copy-start.10
  169.8 0.7 copy-start.19
  169.8 1.0 copy-start.11
  169.8 1.9 copy-start.4
  435.4 2.8 copy-start.2
  438.3 1.0 copy-start.8
  438.3 1.9 copy-start.1
Sparse Core Ops, SparseCore 0:
  9.7 54.7 all-gather.4
  170.0 249.7 all-gather.6
